TPU v7x, 32 devices: a whole 2x2x4 slice. The times are simulated.
32 devices in a mesh: blk: 4 (over z), head: 2 (over core), clip: 4 (over y, x).
Axes of the slice: x: 2, y: 2, z: 4, core: 2. Of those that a mesh axis runs over, the one named last changes fastest.
Arguments:
- tokens: bfloat16 [4608, 1536], P(('clip', 'blk', 'head')), parts along dimension 0, may hold values from -6 to 6
- modulation: float32 [12, 1536], P('clip'), parts along dimension 0, may hold values from -3 to 3
- w_qkv: bfloat16 [1536, 3, 1536], P(None, None, 'head'), may hold values from -0.25 to 0.25
- w_out: bfloat16 [1536, 1536], P('head'), may hold values from -0.15625 to 0.15625
- w_cross: bfloat16 [1536, 1536], P(None, 'head'), may hold values from -0.15625 to 0.15625
- q_gain: float32 [128], replicated, may hold values from 0.5 to 6
- k_gain: float32 [128], replicated, may hold values from 0.5 to 6
- cross_gain: float32 [128], replicated, may hold values from 0.5 to 6
- scene_keys: bfloat16 [1024, 1536], P(('clip', 'blk'), 'head'), parts along dimension 0, may hold values from -40 to 40
- scene_values: bfloat16 [1024, 1536], P(('clip', 'blk'), 'head'), parts along dimension 0, may hold values from -6 to 6
Outputs:
- hidden: bfloat16 [4608, 1536], P(('clip', 'blk', 'head')), parts along dimension 0
- cross_context: bfloat16 [4608, 1536], P(('clip', 'blk'), 'head'), parts along dimension 0
There are 4 independent parts, one for each index of `clip`. A program takes and returns all parts, laid end to end along the dimension named above; an argument that names none is the same for every part. Nothing has to cross between parts.
All inputs are finite; a program needn't handle non-finite values.
Results may differ from a plain program's by a relative error of at most 0.015.
The roundings to bfloat16 on the way count: a program that leaves them out, or rounds other values in their place, can miss the bound.
Values may be sent and summed in bfloat16 or wider, within the bound.
No kernel may reach another device: no remote copies, remote signals or barrier semaphores. Data moves between devices by JAX's collectives and lax.ppermute only.
A program may use at most 128 MiB of HBM per device.

v0:
```python
import jax
import jax.numpy as jnp
from jax import lax
from jax.sharding import PartitionSpec as P

HD = 128


def head_norm(values, gain):
    rms = jnp.mean(values * values, axis=-1, keepdims=True)
    return values * lax.rsqrt(rms + 1e-06) * gain


def attend_block(carry, queries, keys_blk, values_blk):
    best, total, accum = carry
    count = keys_blk.shape[0]
    heads_here = queries.shape[1]
    width = queries.shape[2]
    keys_three = keys_blk.reshape(count, heads_here, width)
    values_three = values_blk.reshape(count, heads_here, width).astype(jnp.float32)
    scores = jnp.einsum("rhd,nhd->hrn", queries, keys_three, preferred_element_type=jnp.float32) * (
        1.0 / width**0.5
    )
    newbest = jnp.maximum(best, jnp.max(scores, axis=-1))
    factor = jnp.exp(best - newbest)
    weights = jnp.exp(scores - newbest[..., None])
    total = total * factor + jnp.sum(weights, axis=-1)
    accum = accum * jnp.transpose(factor)[..., None] + jnp.einsum(
        "hrn,nhd->rhd", weights, values_three
    )
    return (newbest, total, accum)


def attend_keys(carry, queries, keys_rows, values_rows):
    count = keys_rows.shape[0]
    if count > 1024 and count % 1024 == 0:
        blocks = count // 1024
        keys_split = keys_rows.reshape(blocks, 1024, keys_rows.shape[1])
        values_split = values_rows.reshape(blocks, 1024, values_rows.shape[1])

        def advance(state, pair):
            return (attend_block(state, queries, pair[0], pair[1]), None)

        carry, unused = lax.scan(advance, carry, (keys_split, values_split))
        return carry
    return attend_block(carry, queries, keys_rows, values_rows)


def start_state(queries):
    rows = queries.shape[0]
    heads_here = queries.shape[1]
    best = jnp.full((heads_here, rows), -1e30, jnp.float32)
    total = jnp.zeros((heads_here, rows), jnp.float32)
    accum = jnp.zeros(queries.shape, jnp.float32)
    return (best, total, accum)


def finish_state(state):
    best, total, accum = state
    result = accum / jnp.transpose(total)[..., None]
    return result.reshape(result.shape[0], result.shape[1] * result.shape[2]).astype(jnp.bfloat16)


def shards(
    tokens, modulation, w_qkv, w_out, w_cross, q_gain, k_gain, cross_gain, scene_keys, scene_values
):
    width = tokens.shape[1]
    local_width = w_qkv.shape[2]
    heads_here = local_width // HD
    rows_raw = lax.all_gather(tokens, "head", axis=0, tiled=True)
    rows_count = rows_raw.shape[0]
    xfloat = rows_raw.astype(jnp.float32)
    mean = jnp.mean(xfloat, axis=-1, keepdims=True)
    var = jnp.mean((xfloat - mean) ** 2, axis=-1, keepdims=True)
    normed = (xfloat - mean) * lax.rsqrt(var + 1e-06)
    modulated = (normed * (1.0 + modulation[1]) + modulation[0]).astype(jnp.bfloat16)
    projected = jnp.dot(
        modulated, w_qkv.reshape(width, 3 * local_width), preferred_element_type=jnp.float32
    )
    projected = projected.reshape(rows_count, 3, heads_here, HD)
    queries = head_norm(projected[:, 0], q_gain).astype(jnp.bfloat16)
    keys_flat = (
        head_norm(projected[:, 1], k_gain).astype(jnp.bfloat16).reshape(rows_count, local_width)
    )
    values_flat = projected[:, 2].astype(jnp.bfloat16).reshape(rows_count, local_width)
    pieces = (
        lax.all_gather(keys_flat, "blk", axis=0, tiled=True),
        lax.all_gather(values_flat, "blk", axis=0, tiled=True),
    )
    state = attend_keys(start_state(queries), queries, pieces[0], pieces[1])
    context = finish_state(state)
    partial_sum = jnp.dot(context, w_out, preferred_element_type=jnp.float32)
    mine = lax.psum_scatter(partial_sum, "head", scatter_dimension=0, tiled=True)
    hidden = (tokens.astype(jnp.float32) + modulation[2] * mine).astype(jnp.bfloat16)
    hidden_all = lax.all_gather(hidden, "head", axis=0, tiled=True)
    cross_proj = jnp.dot(hidden_all, w_cross, preferred_element_type=jnp.float32).reshape(
        rows_count, heads_here, HD
    )
    cross_queries = head_norm(cross_proj, cross_gain).astype(jnp.bfloat16)
    pieces = (
        lax.all_gather(scene_keys, "blk", axis=0, tiled=True),
        lax.all_gather(scene_values, "blk", axis=0, tiled=True),
    )
    scene_state = attend_keys(start_state(cross_queries), cross_queries, pieces[0], pieces[1])
    cross_context = finish_state(scene_state)
    return (hidden, cross_context)


def solution(mesh):
    return jax.shard_map(
        shards,
        mesh=mesh,
        in_specs=(
            P(("clip", "blk", "head"), None),
            P("clip", None),
            P(None, None, "head"),
            P("head", None),
            P(None, "head"),
            P(),
            P(),
            P(),
            P(("clip", "blk"), "head"),
            P(("clip", "blk"), "head"),
        ),
        out_specs=(P(("clip", "blk", "head"), None), P(("clip", "blk"), "head")),
        check_vma=False,
    )
```

profile of v0, /device:TPU:0, one launch (start us, length us, event | category | flops | bytes accessed | tf_op | source)
XLA Modules:
  0.0 181.9 jit_solution(1748630479518706990)
XLA Ops:
  7.2 2.9 %all_gather.18 = bf16[288,1536]{1,0:T(8,128)(2,1)S(1)} all-gather(bf16[144,1536]{1,0:T(8,128)(2,1)} %param.10), channel_id=1, replica_groups=mesh['blk'=4,'head'=2,'clip'=4] {'head'}, dimensions={0}, use_global_device_ids=true | all-gather | bytes 1327104 | tf_op jit(solution)/shard_map/all_gather | solution.py:70
  10.8 10.3 %copy.45 = bf16[1536,3,768]{0,2,1:T(8,128)(2,1)} copy(bf16[1536,3,768]{2,0,1:T(8,128)(2,1)} %param.12) | data formatting | bytes 14155776 | tf_op args[2]
  21.1 5.0 %fusion.23 = f32[288,3,6,128]{3,0,2,1:T(8,128)S(1)} fusion(bf16[3,6,128,1536]{3,2,1,0:T(8,128)(2,1)} %bitcast.93, bf16[288,1536]{1,0:T(8,128)(2,1)S(1)} %all_gather.18, f32[1536]{0:T(1024)S(1)} %get-tuple-element.3, f32[1536]{0:T(1024)S(1)} %get-tuple-element.4, f32[288]{0:T(512)S(1)} %add_rsqrt_fusion.3, f32[288]{0:T(512)S(1)} %broadcast_multiply_fusion), kind=kOutput, calls=%fused_computation.31 | convolution fusion | flops 2041085952 | bytes 10631424 | tf_op jit(solution)/shard_map/dot_general | solution.py:77
  26.1 1.5 copy-done.2
  29.1 1.0 fusion.26
  30.2 1.2 slice.39
  31.7 0.8 copy.84
  32.6 1.6 multiply_reduce_fusion.4
  34.1 39.0 %all-gather.3.cloned.1.call-done = bf16[1152,768]{1,0:T(8,128)(2,1)} async-done(((bf16[288,768]{1,0:T(8,128)(2,1)}), bf16[1152,768]{1,0:T(8,128)(2,1)}) %all-gather.3.cloned.1.call-update) | async-done | bytes 1769488 | tf_op jit(solution)/shard_map/all_gather | solution.py:87
  73.2 3.9 %copy.48 = bf16[1152,768]{0,1:T(8,128)(2,1)} copy(bf16[1152,768]{1,0:T(8,128)(2,1)} %all-gather.3.cloned.1.call-done) | data formatting | bytes 3538944 | tf_op jit(solution)/shard_map/all_gather | solution.py:87
  77.0 3.1 %multiply_reduce_fusion = (f32[6,288]{1,0:T(8,128)S(1)}, f32[6,288,1152]{2,1,0:T(8,128)S(1)}) fusion(bf16[1152,6,128]{0,2,1:T(8,128)(2,1)} %bitcast.94, f32[288,3,6,128]{3,0,2,1:T(8,128)} %copy-done.2, f32[128]{0:T(128)S(1)} %copy-done.10, f32[288,6]{0,1:T(8,128)S(1)} %add_rsqrt_fusion.2), kind=kOutput, calls=%fused_computation.1 | convolution fusion | flops 514251072 | bytes 10631168 | tf_op jit(solution)/shard_map/rhd,nhd->hrn/dot_general | solution.py:21
  80.2 1.8 %fusion = f32[6,288]{1,0:T(8,128)S(1)} fusion(f32[6,288,1152]{2,1,0:T(8,128)S(1)} %get-tuple-element.12, f32[6,288]{1,0:T(8,128)S(1)} %get-tuple-element.10), kind=kLoop, calls=%fused_computation.2 | loop fusion | flops 5970240 | bytes 7976448 | tf_op jit(solution)/shard_map/reduce_sum | solution.py:27
  82.0 1.2 copy-done.1
  83.3 31.2 %all-gather.5.cloned.1.call-done = bf16[1152,768]{1,0:T(8,128)(2,1)} async-done(((bf16[288,768]{1,0:T(8,128)(2,1)}), bf16[1152,768]{1,0:T(8,128)(2,1)}) %all-gather.5.cloned.1.call-update) | async-done | bytes 1769488 | tf_op jit(solution)/shard_map/all_gather | solution.py:88
  114.4 3.9 %copy.51 = bf16[1152,768]{0,1:T(8,128)(2,1)} copy(bf16[1152,768]{1,0:T(8,128)(2,1)} %all-gather.5.cloned.1.call-done) | data formatting | bytes 3538944 | tf_op jit(solution)/shard_map/all_gather | solution.py:88
  118.3 5.4 %fusion.21 = bf16[6,36,8,128]{3,2,1,0:T(8,128)(2,1)S(1)} fusion(bf16[1152,6,128]{0,2,1:T(8,128)(2,1)} %bitcast.98, f32[6,288,1152]{2,1,0:T(8,128)} %copy-done.1, f32[6,288]{1,0:T(8,128)S(1)} %get-tuple-element.10, f32[288,6]{0,1:T(8,128)S(1)} %bitcast_add_fusion.1, f32[288,6]{0,1:T(8,128)S(1)} %get-tuple-element.9), kind=kOutput, calls=%fused_computation.29 | convolution fusion | flops 514252800 | bytes 10195200 | tf_op jit(solution)/shard_map/hrn,nhd->rhd/dot_general | solution.py:28
  123.7 2.1 %fusion.34 = f32[288,1536]{1,0:T(8,128)} fusion(bf16[768,1536]{1,0:T(8,128)(2,1)S(1)} %copy-done, bf16[6,36,8,128]{3,2,1,0:T(8,128)(2,1)S(1)} %fusion.21), kind=kOutput, calls=%fused_computation.50 | convolution fusion | flops 679477248 | bytes 4571136 | tf_op jit(solution)/shard_map/dot_general | solution.py:92
  125.8 0.9 copy-done.7
  126.7 15.4 %all_gather.22 = bf16[256,768]{1,0:T(8,128)(2,1)S(1)} all-gather(bf16[64,768]{1,0:T(8,128)(2,1)S(1)} %copy-done.7), channel_id=1, replica_groups=mesh['blk'=4,'head'=2,'clip'=4] {'blk'}, dimensions={0}, use_global_device_ids=true | all-gather | bytes 491520 | tf_op jit(solution)/shard_map/all_gather | solution.py:101
  142.1 0.9 copy.56
  143.0 14.9 %all_gather.23 = bf16[256,768]{1,0:T(8,128)(2,1)S(1)} all-gather(bf16[64,768]{1,0:T(8,128)(2,1)S(1)} %copy-done.8), channel_id=1, replica_groups=mesh['blk'=4,'head'=2,'clip'=4] {'blk'}, dimensions={0}, use_global_device_ids=true | all-gather | bytes 491520 | tf_op jit(solution)/shard_map/all_gather | solution.py:102
  157.9 0.9 copy.59
  158.9 1.4 add_convert_fusion
  161.1 2.6 %all_gather.21 = bf16[288,1536]{1,0:T(8,128)(2,1)S(1)} all-gather(bf16[144,1536]{1,0:T(8,128)(2,1)S(1)} %add_convert_fusion), channel_id=1, replica_groups=mesh['blk'=4,'head'=2,'clip'=4] {'head'}, dimensions={0}, use_global_device_ids=true | all-gather | bytes 1327104 | tf_op jit(solution)/shard_map/all_gather | solution.py:95
  163.7 1.8 fusion.44
  165.5 1.3 reshape.88
  166.8 1.0 multiply_reduce_fusion.2
  167.8 1.0 copy.54
  169.4 1.5 copy.55
  170.9 1.3 multiply_convert_fusion
  173.6 0.9 fusion.18
  174.5 0.8 copy.85
  (52 shorter events, 5.2 us)
Async XLA Ops:
  7.2 116.6 %copy-start = (bf16[768,1536]{1,0:T(8,128)(2,1)S(1)}, bf16[768,1536]{1,0:T(8,128)(2,1)}, u32[]{:S(2)}) copy-start(bf16[768,1536]{1,0:T(8,128)(2,1)} %param.13) | copy-start | bytes 7077892
  7.2 3.6 %copy-start.9 = (f32[3,1536]{1,0:T(4,128)S(1)}, f32[3,1536]{1,0:T(4,128)}, u32[]{:S(2)}) copy-start(f32[3,1536]{1,0:T(4,128)} %param.11) | copy-start | bytes 55300
  7.2 66.0 %all-gather.3.cloned.1.call-start = ((), (), s32[]{:S(2)}) async-start(), calls=%async_computation.1 | async-start | bytes 2211840 | tf_op jit(solution)/shard_map/all_gather | solution.py:87
  26.1 1.5 copy-start.2
  27.6 1.1 copy-start.12
  30.2 84.3 %all-gather.5.cloned.1.call-start = ((), (), s32[]{:S(2)}) async-start(), calls=%async_computation.2 | async-start | bytes 2211840 | tf_op jit(solution)/shard_map/all_gather | solution.py:88
  32.5 126.4 %reduce-scatter.2.cloned.1.call-start = ((), (), s32[]{:S(2)}) async-start(), calls=%async_computation.3 | async-start | bytes 2654208 | tf_op jit(solution)/shard_map/reduce_scatter | solution.py:93
  34.1 42.9 %copy-start.10 = (f32[128]{0:T(128)S(1)}, f32[128]{0:T(128)}, u32[]{:S(2)}) copy-start(f32[128]{0:T(128)} %param.15) | copy-start | bytes 1540
  80.2 3.1 %copy-start.1 = (f32[6,288,1152]{2,1,0:T(8,128)}, f32[6,288,1152]{2,1,0:T(8,128)S(1)}, u32[]{:S(2)}) copy-start(f32[6,288,1152]{2,1,0:T(8,128)S(1)} %get-tuple-element.12) | copy-start | bytes 23887876
  125.8 0.9 copy-start.7
  125.8 17.2 %copy-start.8 = (bf16[64,768]{1,0:T(8,128)(2,1)S(1)}, bf16[64,768]{1,0:T(8,128)(2,1)}, u32[]{:S(2)}) copy-start(bf16[64,768]{1,0:T(8,128)(2,1)} %param.19) | copy-start | bytes 294916
  125.8 33.1 %copy-start.3 = (bf16[144,1536]{1,0:T(8,128)(2,1)S(1)}, bf16[144,1536]{1,0:T(8,128)(2,1)}, u32[]{:S(2)}) copy-start(bf16[144,1536]{1,0:T(8,128)(2,1)} %param.10) | copy-start | bytes 1327108
  158.9 4.8 %copy-start.13 = (bf16[1536,768]{1,0:T(8,128)(2,1)S(1)}, bf16[1536,768]{1,0:T(8,128)(2,1)}, u32[]{:S(2)}) copy-start(bf16[1536,768]{1,0:T(8,128)(2,1)} %param.14) | copy-start | bytes 7077892
  160.3 0.8 copy-start.4
  165.4 5.5 %copy-start.11 = (f32[128]{0:T(128)S(1)}, f32[128]{0:T(128)}, u32[]{:S(2)}) copy-start(f32[128]{0:T(128)} %param.17) | copy-start | bytes 1540
  170.9 1.3 copy-start.5
  172.3 1.3 copy-start.6
Sparse Core Ops, SparseCore 0:
  30.3 42.8 all-gather.2
  75.3 39.0 all-gather.4
  126.0 8.1 reduce-scatter.1
where the time goes:
time: 183 us; the launch traced here: 182 us
  waiting for transfers between devices  70.3 us (38%)
  blocking collectives  35.8 us (20%)
  local copies, waits for them, and re-layouts  32.2 us (18%)
  matrix products  18.8 us (10%)
  between operations  14 us (8%)
  other arithmetic  10.7 us (6%)
    all_gather x1, waiting for transfers between devices, shards(): lax.all_gather(keys_flat, 'blk', axis=0, tiled=True)  39 us
    all_gather x1, waiting for transfers between devices, shards(): lax.all_gather(values_flat, 'blk', axis=0, tiled=True)  31.2 us
    unnamed x30, local copies, waits for them, and re-layouts  15.5 us
    all_gather x1, blocking collectives, shards(): lax.all_gather(scene_keys, 'blk', axis=0, tiled=True)  15.4 us
    all_gather x1, blocking collectives, shards(): lax.all_gather(scene_values, 'blk', axis=0, tiled=True)  14.9 us
    dot_general x2, matrix products, attend_block(): jnp.einsum('hrn,nhd->rhd', weights, values_three)  6.29 us
    dot_general x1, matrix products, shards(): jnp.dot(modulated, w_qkv.reshape(width, 3 * local_width), preferred_eleme...  4.98 us
    all_gather x1, local copies, waits for them, and re-layouts, shards(): lax.all_gather(values_flat, 'blk', axis=0, tiled=True)  3.88 us
  transfers between devices with their start and end apart: 3, of which 2 were waited for; matrix products, arithmetic and copies ran while one was open for 8% of the time, Pallas kernels for 0%

commit v1 on v0

--- a/solution.py
+++ b/solution.py
@@ -4,6 +4,19 @@
 from jax.sharding import PartitionSpec as P
 
 HD = 128
+
+
+def collect(x, axis, dim):
+    count, index, rows = (lax.axis_size(axis), lax.axis_index(axis), x.shape[dim])
+    right = [(i, (i + 1) % count) for i in range(count)]
+    filled = jnp.zeros((*x.shape[:dim], count * rows, *x.shape[dim + 1 :]), x.dtype)
+    held = x
+    for step in range(count):
+        source = (index - step) % count
+        filled = lax.dynamic_update_slice_in_dim(filled, held, source * rows, axis=dim)
+        if step < count - 1:
+            held = lax.ppermute(held, axis, right)
+    return filled
 
 
 def head_norm(values, gain):
@@ -83,10 +96,7 @@
         head_norm(projected[:, 1], k_gain).astype(jnp.bfloat16).reshape(rows_count, local_width)
     )
     values_flat = projected[:, 2].astype(jnp.bfloat16).reshape(rows_count, local_width)
-    pieces = (
-        lax.all_gather(keys_flat, "blk", axis=0, tiled=True),
-        lax.all_gather(values_flat, "blk", axis=0, tiled=True),
-    )
+    pieces = (lax.all_gather(keys_flat, "blk", axis=0, tiled=True), collect(values_flat, "blk", 0))
     state = attend_keys(start_state(queries), queries, pieces[0], pieces[1])
     context = finish_state(state)
     partial_sum = jnp.dot(context, w_out, preferred_element_type=jnp.float32)

time: 183 us -> 190 us (1.038)
  waiting for transfers between devices: 70.3 us -> 38.1 us
  local copies, waits for them, and re-layouts: 32.2 us -> 59.8 us
  starting transfers between devices: 0.12 us -> 13.5 us
  matrix products: 18.8 us -> 15.3 us
    all_gather x1, waiting for transfers between devices: 39 us -> 0.01 us  [shards(): lax.all_gather(keys_flat, 'blk', axis=0, tiled=True)]
    ppermute x0 -> x3, waiting for transfers between devices: none -> 38 us  [collect(): held = lax.ppermute(held, axis, right)]
    all_gather x1 -> x0, waiting for transfers between devices: 31.2 us -> none  [shards(): lax.all_gather(values_flat, 'blk', axis=0, tiled=True)]
    dynamic_update_slice x0 -> x4, local copies, waits for them, and re-layouts: none -> 28.1 us  [collect(): lax.dynamic_update_slice_in_dim(filled, held, source * rows, axis=dim)]
    ppermute x0 -> x3, starting transfers between devices: none -> 13.4 us  [collect(): held = lax.ppermute(held, axis, right)]
    all_gather x1 -> x0, local copies, waits for them, and re-layouts: 3.88 us -> none  [shards(): lax.all_gather(values_flat, 'blk', axis=0, tiled=True)]
    dot_general x2, matrix products: 6.29 us -> 2.87 us  [attend_block(): jnp.einsum('hrn,nhd->rhd', weights, values_three)]
    ppermute x0 -> x3, local copies, waits for them, and re-layouts: none -> 2.93 us  [collect(): held = lax.ppermute(held, axis, right)]
  transfers between devices with their start and end apart: 3 -> 5, of which waited for: 2 -> 2; matrix products, arithmetic and copies ran while one was open for 8% -> 20% of each run, Pallas kernels for 0% -> 0%
where the time goes in v1:
time: 190 us; the launch traced here: 189 us
  local copies, waits for them, and re-layouts  59.8 us (31%)
  waiting for transfers between devices  38.1 us (20%)
  blocking collectives  36.8 us (19%)
  matrix products  15.3 us (8%)
  between operations  14.4 us (8%)
  starting transfers between devices  13.5 us (7%)
  other arithmetic  10.7 us (6%)
    ppermute x3, waiting for transfers between devices, collect(): held = lax.ppermute(held, axis, right)  38 us
    dynamic_update_slice x4, local copies, waits for them, and re-layouts, collect(): lax.dynamic_update_slice_in_dim(filled, held, source * rows, axis=dim)  28.1 us
    all_gather x1, blocking collectives, shards(): lax.all_gather(scene_keys, 'blk', axis=0, tiled=True)  16.4 us
    all_gather x1, blocking collectives, shards(): lax.all_gather(scene_values, 'blk', axis=0, tiled=True)  15.1 us
    unnamed x34, local copies, waits for them, and re-layouts  14.3 us
    ppermute x3, starting transfers between devices, collect(): held = lax.ppermute(held, axis, right)  13.4 us
    dot_general x1, matrix products, shards(): jnp.dot(modulated, w_qkv.reshape(width, 3 * local_width), preferred_eleme...  4.98 us
    all_gather x1, local copies, waits for them, and re-layouts, shards(): lax.all_gather(keys_flat, 'blk', axis=0, tiled=True)  3.86 us
  transfers between devices with their start and end apart: 5, of which 2 were waited for; matrix products, arithmetic and copies ran while one was open for 20% of the time, Pallas kernels for 0%

profile of v1, /device:TPU:0, one launch (start us, length us, event | category | flops | bytes accessed | tf_op | source)
XLA Modules:
  0.0 188.6 jit_solution(14501841845538203790)
XLA Ops:
  7.2 2.9 %all_gather.15 = bf16[288,1536]{1,0:T(8,128)(2,1)S(1)} all-gather(bf16[144,1536]{1,0:T(8,128)(2,1)} %param.10), channel_id=1, replica_groups=mesh['blk'=4,'head'=2,'clip'=4] {'head'}, dimensions={0}, use_global_device_ids=true | all-gather | bytes 1327104 | tf_op jit(solution)/shard_map/all_gather | solution.py:83
  10.8 10.3 %copy.51 = bf16[1536,3,768]{0,2,1:T(8,128)(2,1)} copy(bf16[1536,3,768]{2,0,1:T(8,128)(2,1)} %param.12) | data formatting | bytes 14155776 | tf_op args[2]
  21.1 5.0 %fusion.23 = f32[288,3,6,128]{3,0,2,1:T(8,128)S(1)} fusion(bf16[3,6,128,1536]{3,2,1,0:T(8,128)(2,1)} %bitcast.93, bf16[288,1536]{1,0:T(8,128)(2,1)S(1)} %all_gather.15, f32[1536]{0:T(1024)S(1)} %get-tuple-element.3, f32[1536]{0:T(1024)S(1)} %get-tuple-element.4, f32[288]{0:T(512)S(1)} %add_rsqrt_fusion.3, f32[288]{0:T(512)S(1)} %broadcast_multiply_fusion), kind=kOutput, calls=%fused_computation.31 | convolution fusion | flops 2041085952 | bytes 10631424 | tf_op jit(solution)/shard_map/dot_general | solution.py:90
  26.1 1.5 copy-done.1
  29.1 1.0 fusion.26
  30.2 1.2 slice.39
  31.7 3.0 %collective-permute-start = (bf16[288,768]{1,0:T(8,128)(2,1)S(1)}, bf16[288,768]{1,0:T(8,128)(2,1)S(1)}, u32[]{:S(2)}, u32[]{:S(2)}) collective-permute-start(bf16[288,768]{1,0:T(8,128)(2,1)S(1)} %bitcast.99), channel_id=1, source_target_pairs={{0,8},{8,16},{16,24},{24,0},{1,9},{9,17},{17,25},{25,1},{2,10},{10... | collective-permute-start | bytes 1327112 | tf_op jit(solution)/shard_map/ppermute | solution.py:18
  34.7 15.2 %collective-permute-done = bf16[288,768]{1,0:T(8,128)(2,1)S(1)} collective-permute-done((bf16[288,768]{1,0:T(8,128)(2,1)S(1)}, bf16[288,768]{1,0:T(8,128)(2,1)S(1)}, u32[]{:S(2)}, u32[]{:S(2)}) %collective-permute-start) | collective-permute-done | bytes 442400 | tf_op jit(solution)/shard_map/ppermute | solution.py:18
  50.7 3.7 %collective-permute-start.1 = (bf16[288,768]{1,0:T(8,128)(2,1)S(1)}, bf16[288,768]{1,0:T(8,128)(2,1)}, u32[]{:S(2)}, u32[]{:S(2)}) collective-permute-start(bf16[288,768]{1,0:T(8,128)(2,1)S(1)} %collective-permute-done), channel_id=1, source_target_pairs={{0,8},{8,16},{16,24},{24,0},{1,9},{9,17},{17,25},{25,1},{2,10},{10... | collective-permute-start | bytes 1327112 | tf_op jit(solution)/shard_map/ppermute | solution.py:18
  54.4 22.8 %collective-permute-done.1 = bf16[288,768]{1,0:T(8,128)(2,1)} collective-permute-done((bf16[288,768]{1,0:T(8,128)(2,1)S(1)}, bf16[288,768]{1,0:T(8,128)(2,1)}, u32[]{:S(2)}, u32[]{:S(2)}) %collective-permute-start.1) | collective-permute-done | bytes 442400 | tf_op jit(solution)/shard_map/ppermute | solution.py:18
  77.2 6.7 %collective-permute-start.2 = (bf16[288,768]{1,0:T(8,128)(2,1)}, bf16[288,768]{1,0:T(8,128)(2,1)}, u32[]{:S(2)}, u32[]{:S(2)}) collective-permute-start(bf16[288,768]{1,0:T(8,128)(2,1)} %collective-permute-done.1), channel_id=1, source_target_pairs={{0,8},{8,16},{16,24},{24,0},{1,9},{9,17},{17,25},{25,1},{2,10},{10... | collective-permute-start | bytes 1327112 | tf_op jit(solution)/shard_map/ppermute | solution.py:18
  84.4 1.3 broadcast_in_dim.2
  85.7 6.7 %dynamic_update_slice.12 = bf16[1152,768]{0,1:T(8,128)(2,1)} dynamic-update-slice(bf16[1152,768]{0,1:T(8,128)(2,1)} %broadcast_in_dim.2, bf16[288,768]{0,1:T(8,128)(2,1)S(1)} %copy.57, s32[]{:T(128)S(6)} %select_n.32, s32[]{:T(128)} %constant.63.clone.1) | dynamic-update-slice | bytes 884740 | tf_op jit(solution)/shard_map/dynamic_update_slice | solution.py:16
  92.4 1.6 multiply_reduce_fusion.4
  94.3 6.7 %dynamic_update_slice.13 = bf16[1152,768]{0,1:T(8,128)(2,1)} dynamic-update-slice(bf16[1152,768]{0,1:T(8,128)(2,1)} %dynamic_update_slice.12, bf16[288,768]{0,1:T(8,128)(2,1)S(1)} %copy.58, s32[]{:T(128)S(6)} %select_n.34, s32[]{:T(128)} %constant.63.clone.1) | dynamic-update-slice | bytes 884740 | tf_op jit(solution)/shard_map/dynamic_update_slice | solution.py:16
  101.0 1.3 copy.59
  102.3 7.3 %dynamic_update_slice.14 = bf16[1152,768]{0,1:T(8,128)(2,1)} dynamic-update-slice(bf16[1152,768]{0,1:T(8,128)(2,1)} %dynamic_update_slice.13, bf16[288,768]{0,1:T(8,128)(2,1)S(1)} %copy.59, s32[]{:T(128)S(6)} %select_n.36, s32[]{:T(128)} %constant.63.clone.1) | dynamic-update-slice | bytes 884740 | tf_op jit(solution)/shard_map/dynamic_update_slice | solution.py:16
  109.6 1.3 copy.60
  111.0 7.4 %dynamic_update_slice.15 = bf16[1152,768]{0,1:T(8,128)(2,1)} dynamic-update-slice(bf16[1152,768]{0,1:T(8,128)(2,1)} %dynamic_update_slice.14, bf16[288,768]{0,1:T(8,128)(2,1)S(1)} %copy.60, s32[]{:T(128)S(6)} %select_n.38, s32[]{:T(128)} %constant.63.clone.1) | dynamic-update-slice | bytes 884740 | tf_op jit(solution)/shard_map/dynamic_update_slice | solution.py:16
  118.3 3.9 %copy.54 = bf16[1152,768]{0,1:T(8,128)(2,1)} copy(bf16[1152,768]{1,0:T(8,128)(2,1)} %all-gather.2.cloned.1.call-done) | data formatting | bytes 3538944 | tf_op jit(solution)/shard_map/all_gather | solution.py:99
  122.2 3.1 %multiply_reduce_fusion = (f32[6,288]{1,0:T(8,128)S(1)}, f32[6,288,1152]{2,1,0:T(8,128)S(1)}) fusion(bf16[1152,6,128]{0,2,1:T(8,128)(2,1)} %bitcast.94, f32[288,3,6,128]{3,0,2,1:T(8,128)} %copy-done.1, f32[128]{0:T(128)S(1)} %copy-done.12, f32[288,6]{0,1:T(8,128)S(1)} %add_rsqrt_fusion.2), kind=kOutput, calls=%fused_computation.1 | convolution fusion | flops 514251072 | bytes 10631168 | tf_op jit(solution)/shard_map/rhd,nhd->hrn/dot_general | solution.py:34
  125.4 1.8 fusion
  127.2 2.0 %fusion.21 = bf16[6,36,8,128]{3,2,1,0:T(8,128)(2,1)S(1)} fusion(bf16[1152,6,128]{0,2,1:T(8,128)(2,1)S(1)} %bitcast.98, f32[6,288,1152]{2,1,0:T(8,128)S(1)} %get-tuple-element.12, f32[6,288]{1,0:T(8,128)S(1)} %get-tuple-element.10, f32[288,6]{0,1:T(8,128)S(1)} %bitcast_add_fusion.1, f32[288,6]{0,1:T(8,128)S(1)} %get-tuple-element.9), kind=kOutput, calls=%fused_computation.29 | convolution fusion | flops 514252800 | bytes 10195200 | tf_op jit(solution)/shard_map/hrn,nhd->rhd/dot_general | solution.py:41
  129.2 2.1 %fusion.34 = f32[288,1536]{1,0:T(8,128)} fusion(bf16[768,1536]{1,0:T(8,128)(2,1)S(1)} %copy-done, bf16[6,36,8,128]{3,2,1,0:T(8,128)(2,1)S(1)} %fusion.21), kind=kOutput, calls=%fused_computation.50 | convolution fusion | flops 679477248 | bytes 4571136 | tf_op jit(solution)/shard_map/dot_general | solution.py:102
  132.1 16.4 %all_gather.18 = bf16[256,768]{1,0:T(8,128)(2,1)S(1)} all-gather(bf16[64,768]{1,0:T(8,128)(2,1)S(1)} %copy-done.9), channel_id=1, replica_groups=mesh['blk'=4,'head'=2,'clip'=4] {'blk'}, dimensions={0}, use_global_device_ids=true | all-gather | bytes 491520 | tf_op jit(solution)/shard_map/all_gather | solution.py:111
  149.5 15.1 %all_gather.19 = bf16[256,768]{1,0:T(8,128)(2,1)S(1)} all-gather(bf16[64,768]{1,0:T(8,128)(2,1)S(1)} %copy-done.10), channel_id=1, replica_groups=mesh['blk'=4,'head'=2,'clip'=4] {'blk'}, dimensions={0}, use_global_device_ids=true | all-gather | bytes 491520 | tf_op jit(solution)/shard_map/all_gather | solution.py:112
  165.4 1.4 add_convert_fusion
  167.6 2.4 %all_gather.17 = bf16[288,1536]{1,0:T(8,128)(2,1)S(1)} all-gather(bf16[144,1536]{1,0:T(8,128)(2,1)S(1)} %add_convert_fusion), channel_id=1, replica_groups=mesh['blk'=4,'head'=2,'clip'=4] {'head'}, dimensions={0}, use_global_device_ids=true | all-gather | bytes 1327104 | tf_op jit(solution)/shard_map/all_gather | solution.py:105
  170.1 1.8 fusion.44
  171.8 1.3 reshape.88
  175.8 1.5 copy.64
  177.3 1.3 multiply_convert_fusion
  (67 shorter events, 13.1 us)
Async XLA Ops:
  7.2 122.0 %copy-start = (bf16[768,1536]{1,0:T(8,128)(2,1)S(1)}, bf16[768,1536]{1,0:T(8,128)(2,1)}, u32[]{:S(2)}) copy-start(bf16[768,1536]{1,0:T(8,128)(2,1)} %param.13) | copy-start | bytes 7077892
  7.2 3.6 %copy-start.11 = (f32[3,1536]{1,0:T(4,128)S(1)}, f32[3,1536]{1,0:T(4,128)}, u32[]{:S(2)}) copy-start(f32[3,1536]{1,0:T(4,128)} %param.11) | copy-start | bytes 55300
  7.2 111.2 %all-gather.2.cloned.1.call-start = ((), (), s32[]{:S(2)}) async-start(), calls=%async_computation.1 | async-start | bytes 2211840 | tf_op jit(solution)/shard_map/all_gather | solution.py:99
  26.1 1.5 copy-start.1
  27.6 1.1 copy-start.14
  30.2 135.3 %reduce-scatter.2.cloned.1.call-start = ((), (), s32[]{:S(2)}) async-start(), calls=%async_computation.2 | async-start | bytes 2654208 | tf_op jit(solution)/shard_map/reduce_scatter | solution.py:103
  31.7 18.2 %collective-permute-start = (bf16[288,768]{1,0:T(8,128)(2,1)S(1)}, bf16[288,768]{1,0:T(8,128)(2,1)S(1)}, u32[]{:S(2)}, u32[]{:S(2)}) collective-permute-start(bf16[288,768]{1,0:T(8,128)(2,1)S(1)} %bitcast.99), channel_id=1, source_target_pairs={{0,8},{8,16},{16,24},{24,0},{1,9},{9,17},{17,25},{25,1},{2,10},{10... | collective-permute-start | bytes 1327112 | tf_op jit(solution)/shard_map/ppermute | solution.py:18
  49.9 0.8 copy-start.6
  50.7 26.6 %collective-permute-start.1 = (bf16[288,768]{1,0:T(8,128)(2,1)S(1)}, bf16[288,768]{1,0:T(8,128)(2,1)}, u32[]{:S(2)}, u32[]{:S(2)}) collective-permute-start(bf16[288,768]{1,0:T(8,128)(2,1)S(1)} %collective-permute-done), channel_id=1, source_target_pairs={{0,8},{8,16},{16,24},{24,0},{1,9},{9,17},{17,25},{25,1},{2,10},{10... | collective-permute-start | bytes 1327112 | tf_op jit(solution)/shard_map/ppermute | solution.py:18
  77.2 32.4 %collective-permute-start.2 = (bf16[288,768]{1,0:T(8,128)(2,1)}, bf16[288,768]{1,0:T(8,128)(2,1)}, u32[]{:S(2)}, u32[]{:S(2)}) collective-permute-start(bf16[288,768]{1,0:T(8,128)(2,1)} %collective-permute-done.1), channel_id=1, source_target_pairs={{0,8},{8,16},{16,24},{24,0},{1,9},{9,17},{17,25},{25,1},{2,10},{10... | collective-permute-start | bytes 1327112 | tf_op jit(solution)/shard_map/ppermute | solution.py:18
  84.4 9.6 %copy-start.7 = (bf16[288,768]{1,0:T(8,128)(2,1)S(1)}, bf16[288,768]{1,0:T(8,128)(2,1)}, u32[]{:S(2)}) copy-start(bf16[288,768]{1,0:T(8,128)(2,1)} %copy-done.6) | copy-start | bytes 1327108
  118.3 3.9 %copy-start.12 = (f32[128]{0:T(128)S(1)}, f32[128]{0:T(128)}, u32[]{:S(2)}) copy-start(f32[128]{0:T(128)} %param.15) | copy-start | bytes 1540
  125.3 1.9 copy-start.4
  131.3 0.9 copy-start.9
  131.3 18.2 %copy-start.10 = (bf16[64,768]{1,0:T(8,128)(2,1)S(1)}, bf16[64,768]{1,0:T(8,128)(2,1)}, u32[]{:S(2)}) copy-start(bf16[64,768]{1,0:T(8,128)(2,1)} %param.19) | copy-start | bytes 294916
  131.3 34.2 %copy-start.2 = (bf16[144,1536]{1,0:T(8,128)(2,1)S(1)}, bf16[144,1536]{1,0:T(8,128)(2,1)}, u32[]{:S(2)}) copy-start(bf16[144,1536]{1,0:T(8,128)(2,1)} %param.10) | copy-start | bytes 1327108
  165.4 4.6 %copy-start.15 = (bf16[1536,768]{1,0:T(8,128)(2,1)S(1)}, bf16[1536,768]{1,0:T(8,128)(2,1)}, u32[]{:S(2)}) copy-start(bf16[1536,768]{1,0:T(8,128)(2,1)} %param.14) | copy-start | bytes 7077892
  166.9 0.8 copy-start.3
  171.8 5.5 %copy-start.13 = (f32[128]{0:T(128)S(1)}, f32[128]{0:T(128)}, u32[]{:S(2)}) copy-start(f32[128]{0:T(128)} %param.17) | copy-start | bytes 1540
  177.3 1.3 copy-start.5
  178.7 1.3 copy-start.8
Sparse Core Ops, SparseCore 0:
  30.3 55.3 all-gather.1
  131.4 10.5 reduce-scatter.1
